TPU v7x, 32 devices: a whole 2x2x4 slice. The times are simulated.
32 devices in a mesh: lon: 8 (over z, x), lat: 4 (over y, core).
Axes of the slice: x: 2, y: 2, z: 4, core: 2. Of those that a mesh axis runs over, the one named last changes fastest.
Arguments:
- thermal_departure: float32 [90, 128, 1024], P(None, 'lat', 'lon'), may hold values from -6 to 6
- moisture_profile: float32 [90, 128, 1024], P(None, 'lat', 'lon'), may hold values from -6 to 6
- solar_elevation_factor: float32 [128, 1024], P('lat', 'lon'), may hold values from 0.1 to 1
- daylight_groups: int32 [128, 8], P('lat', 'lon'), may hold values from 0 to 1, as said below
- spreading_factor: float32 [128, 1024], P('lat', 'lon'), may hold values from 0.03 to 0.24
- entry_layer_matrix: float32 [512, 181], replicated, may hold values from -0.4375 to 0.4375
- entry_layer_offset: float32 [512], replicated, may hold values from -3 to 3
- inner_layer_matrices: float32 [2, 512, 512], replicated, may hold values from -0.25 to 0.25
- inner_layer_offsets: float32 [2, 512], replicated, may hold values from -3 to 3
- final_layer_matrix: float32 [90, 512], replicated, may hold values from -0.25 to 0.25
- final_layer_offset: float32 [90], replicated, may hold values from -3 to 3
Outputs:
- heating: float32 [90, 128, 1024], P(None, 'lat', 'lon')
- temp_next: float32 [90, 128, 1024], P(None, 'lat', 'lon')
Inputs may be any that keep to these rules, and one draw needn't show every extreme that they name: In every row the sunlit strips form one run of 4 consecutive strips, wrapping around, so daylight_groups[r, j] + daylight_groups[r, (j + 4) mod 8] == 1; row r and row r + 32 are complements of each other.
All inputs are finite; a program needn't handle non-finite values.
Results may differ from a plain program's by a relative error of at most 0.0001.
Values sent between devices are 32-bit elements; how exact they have to be, the bound alone decides.
A program may use at most 64 MiB of HBM per device.

v0:
```python
import jax
import jax.numpy as jnp
from jax import lax
from jax.experimental import pallas as pl
from jax.experimental.pallas import tpu as pltpu
from jax.sharding import PartitionSpec as P

MESH = pl.DeviceIdType.MESH
GROUP = 4
EDGE = 4
CHUNKS = 2
PAD = 8


def up8(n):
    return (n + 7) // 8 * 8


def split(x):
    hi = x.astype(jnp.bfloat16)
    lo = (x - hi.astype(jnp.float32)).astype(jnp.bfloat16)
    return hi, lo


def dot(a, b):
    return jnp.dot(a, b, preferred_element_type=jnp.float32)


def dot3(w_hi, w_lo, x):
    hi, lo = split(x)
    return dot(w_hi, hi) + dot(w_hi, lo) + dot(w_lo, hi)


def gate(h):
    return h + h * jnp.tanh(h)


def roll(x, shift, axis):
    return pltpu.roll(x, shift % x.shape[axis], axis)


def kernel(
    temp, moist, mu, lit_h, spread, w0t_h, b0_h, wm_h, bm_h, wf_h, bf_h,
    heat, nxt,
    lit, w0t, b0, wm, bm, wf, bf,
    temp_v, moist_v, mu_v, spread_v, temp_r, moist_r, mu_r,
    w0_hi, w0_lo, wm_hi, wm_lo, wf_hi, wf_lo, b0_c, bm_c, bf_c,
    xs, res, res_r,
    temp_t, temp_b, spread_t, spread_b,
    pack, left_m, left_t, left_b, right_m, right_t, right_b,
    edge_0, edge_1, f_all,
    in_sem, send_sem, recv_sem, out_send, out_recv, halo_send, halo_recv,
):
    levels, rows, lanes = temp.shape
    half = rows // 2
    hid = wm_h.shape[1]
    depth = wm_h.shape[0]
    groups = half // GROUP
    lp = up8(levels)
    tiles = pack.shape[0] - 1
    slots = lanes // EDGE
    n_lat = lax.axis_size("lat")
    n_lon = lax.axis_size("lon")
    lat = lax.axis_index("lat")
    lon = lax.axis_index("lon")
    parity = lax.rem(lat, 2)
    partner = lat + 1 - 2 * parity
    mine = pl.multiple_of(parity * half, half)
    theirs = pl.multiple_of(half - parity * half, half)
    left = lax.rem(lon + n_lon - 1, n_lon)
    right = lax.rem(lon + 1, n_lon)
    has_up = lat > 0
    has_down = lat < n_lat - 1
    up = jnp.maximum(lat - 1, 0)
    down = jnp.minimum(lat + 1, n_lat - 1)

    own = [
        pltpu.make_async_copy(src, dst, in_sem.at[i])
        for i, (src, dst) in enumerate((
            (temp, temp_v), (spread, spread_v), (w0t_h, w0t), (wm_h, wm), (wf_h, wf),
            (b0_h, b0), (bm_h, bm), (bf_h, bf), (mu, mu_v), (lit_h, lit), (moist, moist_v)))
    ]
    def at(lat_to, lon_to):
        return {"lat": lat_to, "lon": lon_to}

    barrier = pltpu.get_barrier_semaphore()

    def hello(lat_to, lon_to):
        pl.semaphore_signal(barrier, inc=1, device_id=at(lat_to, lon_to), device_id_type=MESH)

    hello(lat, left)
    hello(lat, right)

    @pl.when(has_up)
    def _():
        for to in (left, lon, right):
            hello(up, to)

    @pl.when(has_down)
    def _():
        for to in (left, lon, right):
            hello(down, to)

    for copy in own:
        copy.start()

    first, last = pl.ds(0, PAD), pl.ds(rows - PAD, PAD)

    def halo(i, src, dst, lat_to, lon_to):
        return pltpu.make_async_remote_copy(
            src_ref=src, dst_ref=dst, send_sem=halo_send.at[i], recv_sem=halo_recv.at[i],
            device_id=at(lat_to, lon_to), device_id_type=MESH)

    beside = [
        halo(0, pack, right_m, lat, left),
        halo(1, pack, left_m, lat, right),
    ]
    to_up = [
        halo(2, spread.at[first, :], spread_b, up, lon),
        halo(3, temp.at[:, first, :], temp_b, up, lon),
        halo(4, pack.at[:, first, :], right_b, up, left),
        halo(5, pack.at[:, first, :], left_b, up, right),
    ]
    to_down = [
        halo(6, spread.at[last, :], spread_t, down, lon),
        halo(7, temp.at[:, last, :], temp_t, down, lon),
        halo(8, pack.at[:, last, :], right_t, down, left),
        halo(9, pack.at[:, last, :], left_t, down, right),
    ]

    for copy in own[:2]:
        copy.wait()
    lane = lax.broadcasted_iota(jnp.int32, (rows, lanes), 1)
    for t in range(tiles):
        count = min(slots, levels - t * slots)
        acc = jnp.zeros((rows, lanes), jnp.float32)
        for m in range(count):
            moved = roll(temp_v[t * slots + m], EDGE * m + 2, 1)
            acc = jnp.where(lane // EDGE == m, moved, acc)
        pack[t] = acc
    acc = jnp.where(lane < EDGE, roll(spread_v[...], 2, 1), 0.0)
    step = EDGE
    while step < lanes:
        acc = acc + roll(acc, step, 1)
        step *= 2
    pack[tiles] = acc

    @pl.when(jnp.logical_not(has_up))
    def _():
        for ref in (temp_t, spread_t, left_t, right_t):
            ref[...] = jnp.zeros_like(ref)

    @pl.when(jnp.logical_not(has_down))
    def _():
        for ref in (temp_b, spread_b, left_b, right_b):
            ref[...] = jnp.zeros_like(ref)

    for copy in own[2:]:
        copy.wait()

    xs[...] = jnp.zeros_like(xs)
    xs[0:levels, 0:hid] = w0t[0:levels, :] * 0.5
    xs[lp:lp + levels, 0:hid] = w0t[levels:2 * levels, :] * 0.5
    xs[2 * lp:2 * lp + 1, 0:hid] = w0t[2 * levels:2 * levels + 1, :] * 0.5
    w0_hi[...], w0_lo[...] = split(xs[:, 0:hid].T)
    for k in range(depth):
        wm_hi[k], wm_lo[k] = split(wm[k] * 0.5)
    wf_hi[...], wf_lo[...] = split(wf[...])

    def column(row):
        return jnp.broadcast_to(row, (lanes, row.shape[1])).T

    b0_c[...] = column(b0[...] * 0.5)
    for k in range(depth):
        bm_c[k] = column(bm[k:k + 1, :] * 0.5)
    bf_c[...] = column(bf[...])
    xs[...] = jnp.zeros_like(xs)

    pl.semaphore_wait(
        barrier, 2 + 3 * has_up.astype(jnp.int32) + 3 * has_down.astype(jnp.int32))

    chunk = half // CHUNKS

    def swap(i, src, dst):
        return pltpu.make_async_remote_copy(
            src_ref=src, dst_ref=dst, send_sem=send_sem.at[i], recv_sem=recv_sem.at[i],
            device_id=at(partner, lon), device_id_type=MESH)

    out = []
    for c in range(CHUNKS):
        theirs_c = pl.ds(pl.multiple_of(theirs + c * chunk, chunk), chunk)
        here_c = pl.ds(c * chunk, chunk)
        out.append([
            swap(3 * c, temp.at[:, theirs_c, :], temp_r.at[:, here_c, :]),
            swap(3 * c + 1, moist.at[:, theirs_c, :], moist_r.at[:, here_c, :]),
            swap(3 * c + 2, mu.at[theirs_c, :], mu_r.at[here_c, :]),
        ])

    for copy in out[0] + beside:
        copy.start()

    @pl.when(has_up)
    def _():
        for copy in to_up:
            copy.start()

    @pl.when(has_down)
    def _():
        for copy in to_down:
            copy.start()

    for later in out[1:]:
        for copy in later:
            copy.start()


    temp_f = temp_v.reshape(levels * rows, lanes)
    moist_f = moist_v.reshape(levels * rows, lanes)
    temp_rf = temp_r.reshape(levels * half, lanes)
    moist_rf = moist_r.reshape(levels * half, lanes)

    def wide(c):
        return jnp.concatenate([c] * GROUP, axis=1)

    def send(g):
        rows_g = pl.ds(g * GROUP, GROUP)
        return pltpu.make_async_remote_copy(
            src_ref=res.at[rows_g], dst_ref=res_r.at[rows_g],
            send_sem=out_send.at[g], recv_sem=out_recv.at[g],
            device_id=at(partner, lon), device_id_type=MESH)

    heat_f = heat.reshape(levels * rows, lanes)

    def place_row(r, value):
        heat_f[pl.ds(r, levels, stride=rows), :] = value * lit[r].astype(jnp.float32)

    def network(g, beside_it=lambda part: None):
        for j in range(GROUP):
            i = g * GROUP + j
            r = mine + i
            on = lit[r].astype(jnp.float32)
            off = 1.0 - on
            cols = slice(j * lanes, (j + 1) * lanes)
            xs[0:levels, cols] = (
                temp_f[pl.ds(r, levels, stride=rows), :] * on
                + temp_rf[pl.ds(i, levels, stride=half), :] * off)
            xs[lp:lp + levels, cols] = (
                moist_f[pl.ds(r, levels, stride=rows), :] * on
                + moist_rf[pl.ds(i, levels, stride=half), :] * off)
            xs[2 * lp:2 * lp + 1, cols] = (
                mu_v[pl.ds(r, 1), :] * on + mu_r[pl.ds(i, 1), :] * off)
        h = gate(dot3(w0_hi[...], w0_lo[...], xs[...]) + wide(b0_c[...]))
        beside_it(0)
        for k in range(depth):
            h = gate(dot3(wm_hi[k], wm_lo[k], h) + wide(bm_c[k]))
            beside_it(1 + k)
        y = dot3(wf_hi[...], wf_lo[...], h) + wide(bf_c[...])
        y = y * xs[2 * lp:2 * lp + 1, :]
        for j in range(GROUP):
            value = y[:, j * lanes:(j + 1) * lanes]
            res[g * GROUP + j] = value
            place_row(mine + g * GROUP + j, value)
        send(g).start()

    def arrive(c):
        for copy in out[c]:
            copy.wait()

    arrive(0)
    network(0)

    for copy in beside:
        copy.wait()

    @pl.when(has_up)
    def _():
        for copy in to_up:
            copy.wait_send()
        for copy in to_down:
            copy.wait_recv()

    @pl.when(has_down)
    def _():
        for copy in to_down:
            copy.wait_send()
        for copy in to_up:
            copy.wait_recv()

    tall = rows + 2 * PAD

    def stack(top, middle, bottom):
        return jnp.concatenate([top, middle, bottom], axis=0)

    def advance(x, f, west, east):
        beside = roll(x, 1, 0) + roll(x, x.shape[0] - 1, 0) + west + east
        return x + f * (beside - 4.0 * x)

    slot = lax.broadcasted_iota(jnp.int32, (tall, lanes), 1)
    place = lax.rem(slot, EDGE)
    zero8 = jnp.zeros((PAD, lanes), jnp.float32)

    def gather(t):
        lhs = stack(left_t[t], left_m[t], left_b[t])
        rhs = stack(right_t[t], right_m[t], right_b[t])
        here = stack(zero8, pack[t], zero8)
        return (jnp.where(place < 2, lhs, here), jnp.where(place < 2, here, rhs))

    f_west, f_east = gather(tiles)
    for t in range(tiles):
        west, east = gather(t)
        edge_0[t] = jnp.where(place == 1, roll(east, lanes - 1, 1), roll(west, 1, 1))
        west = advance(west, f_west, roll(west, 1, 1), roll(west, lanes - 1, 1))
        east = advance(east, f_east, roll(east, 1, 1), roll(east, lanes - 1, 1))
        edge_1[t] = jnp.where(place == 1, roll(east, lanes - 1, 1), roll(west, 1, 1))

    f_all[...] = stack(spread_t[...], spread_v[...], spread_b[...])
    def diffuse(k):
        t, m = k // slots, lax.rem(k, slots)
        turn = lanes - 2 - EDGE * m
        x = stack(temp_t[k], temp_v[k], temp_b[k])
        rim = pltpu.roll(edge_0[t], turn, 1)
        west = jnp.where(slot == 0, rim, roll(x, 1, 1))
        east = jnp.where(slot == lanes - 1, rim, roll(x, lanes - 1, 1))
        x = advance(x, f_all[...], west, east)
        core = x[PAD:PAD + rows]
        rim = pltpu.roll(edge_1[t, PAD:PAD + rows], turn, 1)
        place = slot[PAD:PAD + rows]
        west = jnp.where(place == 0, rim, roll(core, 1, 1))
        east = jnp.where(place == lanes - 1, rim, roll(core, lanes - 1, 1))
        above, below = roll(x, 1, 0)[PAD:PAD + rows], roll(x, tall - 1, 0)[PAD:PAD + rows]
        beside = above + below + west + east
        nxt[k] = core + spread_v[...] * (beside - 4.0 * core)

    per = levels // (groups - 1)
    parts = depth + 1

    def both(g, carry):
        @pl.when(g == groups // CHUNKS)
        def _():
            arrive(1)

        begin = (g - 1) * per

        def some(part):
            for k in range(per * part // parts, per * (part + 1) // parts):
                diffuse(begin + k)

        network(g, some)
        return carry

    lax.fori_loop(1, groups, both, 0)
    for k in range(per * (groups - 1), levels):
        diffuse(jnp.int32(k))

    for g in range(half // GROUP):
        send(g).wait()
    for i in range(half):
        place_row(theirs + i, res_r[i])


def run(temp, moist, mu, lit, spread, w0, b0, wm, bm, wf, bf):
    levels, rows, lanes = temp.shape
    half = rows // 2
    hid = wm.shape[1]
    depth = wm.shape[0]
    lp = up8(levels)
    kp = (2 * lp + 256) // 256 * 256
    tall = rows + 2 * PAD
    tiles = (levels * EDGE + lanes - 1) // lanes
    f32, bf16 = jnp.float32, jnp.bfloat16
    vmem = pl.BlockSpec(memory_space=pltpu.VMEM)
    hbm = pl.BlockSpec(memory_space=pltpu.HBM)
    groups = half // GROUP
    dma = pltpu.SemaphoreType.DMA

    def buf(*shape, dtype=f32):
        return pltpu.VMEM(shape, dtype)

    return pl.pallas_call(
        kernel,
        out_shape=(jax.ShapeDtypeStruct(temp.shape, f32),) * 2,
        in_specs=[hbm] * 11,
        out_specs=(vmem, vmem),
        scratch_shapes=[
            pltpu.SMEM((rows,), jnp.int32), buf(*w0.T.shape), buf(1, hid), buf(*wm.shape),
            buf(*bm.shape), buf(*wf.shape), buf(1, levels),
            buf(levels, rows, lanes), buf(levels, rows, lanes), buf(rows, lanes), buf(rows, lanes),
            buf(levels, half, lanes), buf(levels, half, lanes), buf(half, lanes),
            buf(hid, kp, dtype=bf16), buf(hid, kp, dtype=bf16),
            buf(depth, hid, hid, dtype=bf16), buf(depth, hid, hid, dtype=bf16),
            buf(levels, hid, dtype=bf16), buf(levels, hid, dtype=bf16),
            buf(hid, lanes), buf(depth, hid, lanes), buf(levels, lanes),
            buf(kp, max(hid, GROUP * lanes)), buf(half, levels, lanes), buf(half, levels, lanes),
            buf(levels, PAD, lanes), buf(levels, PAD, lanes), buf(PAD, lanes), buf(PAD, lanes),
            buf(tiles + 1, rows, lanes),
            buf(tiles + 1, rows, lanes), buf(tiles + 1, PAD, lanes), buf(tiles + 1, PAD, lanes),
            buf(tiles + 1, rows, lanes), buf(tiles + 1, PAD, lanes), buf(tiles + 1, PAD, lanes),
            buf(tiles, tall, lanes), buf(tiles, tall, lanes), buf(tall, lanes),
            dma((11,)), dma((3 * CHUNKS,)), dma((3 * CHUNKS,)), dma((groups,)), dma((groups,)),
            dma((10,)), dma((10,)),
        ],
        compiler_params=pltpu.CompilerParams(
            collective_id=0, has_side_effects=True, vmem_limit_bytes=48 << 20),
    )(*(
        pltpu.with_memory_space_constraint(x, pltpu.HBM)
        for x in (temp, moist, mu, lit, spread, w0.T, b0[None, :], wm, bm, wf, bf[None, :])
    ))


def on_device(
    thermal_departure,
    moisture_profile,
    solar_elevation_factor,
    daylight_groups,
    spreading_factor,
    entry_layer_matrix,
    entry_layer_offset,
    inner_layer_matrices,
    inner_layer_offsets,
    final_layer_matrix,
    final_layer_offset,
):
    heating, state = run(
        thermal_departure,
        moisture_profile,
        solar_elevation_factor,
        daylight_groups[:, 0],
        spreading_factor,
        entry_layer_matrix,
        entry_layer_offset,
        inner_layer_matrices,
        inner_layer_offsets,
        final_layer_matrix,
        final_layer_offset,
    )
    return heating, state + heating


def solution(mesh):
    in_specs = (
        P(None, "lat", "lon"),
        P(None, "lat", "lon"),
        P("lat", "lon"),
        P("lat", "lon"),
        P("lat", "lon"),
        P(),
        P(),
        P(),
        P(),
        P(),
        P(),
    )
    out_specs = (P(None, "lat", "lon"), P(None, "lat", "lon"))
    return jax.shard_map(
        on_device, mesh=mesh, in_specs=in_specs, out_specs=out_specs, check_vma=False
    )
```

profile of v0, /device:TPU:0, one launch (start us, length us, event | category | flops | bytes accessed | tf_op | source)
XLA Modules:
  0.0 29.1 jit_solution(1880700563079663512)
XLA Ops:
  0.6 25.9 %shard_map.122 = (f32[90,32,128]{2,1,0:T(8,128)S(1)}, f32[90,32,128]{2,1,0:T(8,128)S(1)}) custom-call(f32[90,32,128]{2,1,0:T(8,128)} %temp.1, f32[90,32,128]{2,1,0:T(8,128)} %moist.1, f32[32,128]{1,0:T(8,128)} %mu.1, s32[32]{0:T(128)} %bitcast.6, f32[32,128]{1,0:T(8,128)} %spread.1, f32[181,512]{1,0:T(8,128)} %bitcast.4, f32[1,512]{1,0:T(1,128)} %bitcast.5, ...), custom_call_target="tpu_custom_call" | custom-call | tf_op jit(solution)/shard_map/pallas_call | solution.py:379
  26.6 1.4 %add.3 = f32[90,32,128]{2,1,0:T(8,128)} add(f32[90,32,128]{2,1,0:T(8,128)S(1)} %get-tuple-element.5, f32[90,32,128]{2,1,0:T(8,128)S(1)} %get-tuple-element.8) | non-fusion elementwise | flops 368640 | bytes 4423680 | tf_op jit(solution)/shard_map/add | solution.py:436
  28.0 1.1 %copy.14 = f32[90,32,128]{2,1,0:T(8,128)} copy(f32[90,32,128]{2,1,0:T(8,128)S(1)} %get-tuple-element.8) | data formatting | bytes 2949120
where the time goes:
time: 29.3 us; the launch traced here: 29.1 us
  Pallas kernels  25.9 us (88%)
  other arithmetic  1.43 us (5%)
  local copies, waits for them, and re-layouts  1.11 us (4%)
  between operations  0.64 us (2%)
    pallas_call x1, Pallas kernels, run(): pl.pallas_call(kernel, out_shape=(jax.ShapeDtypeStruct(temp.shape, f32),)...  25.9 us
    add x1, other arithmetic, on_device(): return (heating, state + heating)  1.43 us
    unnamed x1, local copies, waits for them, and re-layouts  1.11 us

commit v1 on v0

v1 whole, which is shorter than its diff:
```python
import jax
import jax.numpy as jnp
from jax import lax
from jax.experimental import pallas as pl
from jax.experimental.pallas import tpu as pltpu
from jax.sharding import PartitionSpec as P

MESH = pl.DeviceIdType.MESH
GROUP = 4
EDGE = 4
PAD = 8
REACH = 2
TAIL = 18


def up(n, m):
    return (n + m - 1) // m * m


def split(x):
    hi = x.astype(jnp.bfloat16)
    lo = (x - hi.astype(jnp.float32)).astype(jnp.bfloat16)
    return hi, lo


def dot(a, b):
    return jnp.dot(a, b, preferred_element_type=jnp.float32)


def gate(h):
    return h + h * jnp.tanh(h)


def tall3(x):
    hi, lo = split(x)
    return jnp.concatenate([hi, lo, hi], axis=0)


def wide3(w):
    hi, lo = split(w)
    return jnp.concatenate([hi, hi, lo], axis=1)


def roll(x, shift, axis):
    return pltpu.roll(x, shift % x.shape[axis], axis)


def kernel(
    temp, moist, mu, lit_h, spread, w0t_h, b0_h, wm_h, bm_h, wf_h, bf_h,
    heat, nxt,
    lit, w0t, b0, wm, bm, wf, bf,
    temp_v, spread_v, own_x, far_x,
    w0_p, w0_c, wm_c, wf_c, b0_c, bm_c, bf_c,
    res_own, res_far,
    temp_t, temp_b, spread_t, spread_b,
    pack, left_m, left_t, left_b, right_m, right_t, right_b,
    edge_0, edge_1, f_all,
    in_sem, own_sem, send_sem, recv_sem, put_sem, out_send, out_recv, halo_send, halo_recv,
    pair_sem,
):
    levels, rows, lanes = temp.shape
    half = rows // 2
    hid = wm_h.shape[1]
    depth = wm_h.shape[0]
    groups = half // GROUP
    feat = w0t_h.shape[0]
    kp = w0_c.shape[1] // 3
    tiles = pack.shape[0] - 1
    slots = lanes // EDGE
    n_lat = lax.axis_size("lat")
    n_lon = lax.axis_size("lon")
    lat = lax.axis_index("lat")
    lon = lax.axis_index("lon")
    parity = lax.rem(lat, 2)
    partner = lat + 1 - 2 * parity
    mine = parity * half
    theirs = half - parity * half
    left = lax.rem(lon + n_lon - 1, n_lon)
    right = lax.rem(lon + 1, n_lon)
    has_up = lat > 0
    has_down = lat < n_lat - 1
    above = jnp.maximum(lat - 1, 0)
    below = jnp.minimum(lat + 1, n_lat - 1)
    leads = parity == 1
    pair_up = lat > 1
    pair_down = lat < n_lat - 2

    def at(lat_to, lon_to):
        return {"lat": lat_to, "lon": lon_to}

    def local(i, src, dst):
        return pltpu.make_async_copy(src, dst, in_sem.at[i])

    small = [
        local(0, lit_h, lit), local(1, w0t_h, w0t), local(2, b0_h, b0),
        local(3, bm_h, bm), local(4, bf_h, bf), local(5, spread, spread_v)]
    large = [local(6, wm_h, wm), local(7, wf_h, wf), local(8, temp, temp_v)]

    def own_start(g):
        for i in range(g * GROUP, (g + 1) * GROUP):
            sem = own_sem.at[g]
            r = mine + i
            pltpu.make_async_copy(temp.at[:, r, :], own_x.at[i, pl.ds(0, levels), :], sem).start()
            pltpu.make_async_copy(moist.at[:, r, :], own_x.at[i, pl.ds(levels, levels), :], sem).start()
            pltpu.make_async_copy(
                mu.at[pl.ds(r, 1), :], own_x.at[i, pl.ds(2 * levels, 1), :], sem).start()

    def group_of(ref, g, count):
        return ref.at[pl.ds(g * GROUP, GROUP), pl.ds(0, count), :]

    def own_wait(g):
        block = group_of(own_x, g, feat)
        pltpu.make_async_copy(block, block, own_sem.at[g]).wait()

    def swap(g, src, dst):
        return pltpu.make_async_remote_copy(
            src_ref=src, dst_ref=dst, send_sem=send_sem.at[g], recv_sem=recv_sem.at[g],
            device_id=at(partner, lon), device_id_type=MESH)

    def far_start(g):
        for i in range(g * GROUP, (g + 1) * GROUP):
            r = theirs + i
            swap(g, temp.at[:, r, :], far_x.at[i, pl.ds(0, levels), :]).start()
            swap(g, moist.at[:, r, :], far_x.at[i, pl.ds(levels, levels), :]).start()
            swap(g, mu.at[pl.ds(r, 1), :], far_x.at[i, pl.ds(2 * levels, 1), :]).start()

    def far_wait(g):
        block = group_of(far_x, g, feat)
        swap(g, block, block).wait()

    barrier = pltpu.get_barrier_semaphore()

    for copy in small:
        copy.start()

    @pl.when(leads)
    def _():
        pl.semaphore_signal(barrier, inc=1, device_id=at(partner, lon), device_id_type=MESH)

    own_start(0)
    own_start(1)

    @pl.when(jnp.logical_not(leads))
    def _():
        pl.semaphore_wait(barrier, 1)
        pl.semaphore_signal(pair_sem, inc=1, device_id=at(partner, lon), device_id_type=MESH)

    @pl.when(leads)
    def _():
        pl.semaphore_wait(pair_sem, 1)

        def hello(lat_to, lon_to):
            pl.semaphore_signal(
                barrier, inc=1, device_id=at(lat_to, lon_to), device_id_type=MESH)

        hello(lat, left)
        hello(lat, right)

        @pl.when(pair_up)
        def _():
            for to in (left, lon, right):
                hello(jnp.maximum(lat - 2, 0), to)

        @pl.when(pair_down)
        def _():
            for to in (left, lon, right):
                hello(jnp.minimum(lat + 2, n_lat - 1), to)

    far_start(0)
    far_start(1)
    large[0].start()
    large[1].start()
    large[2].start()
    for g in range(2, groups):
        far_start(g)
        own_start(g)

    first, last = pl.ds(0, PAD), pl.ds(rows - PAD, PAD)

    def halo(i, src, dst, lat_to, lon_to):
        return pltpu.make_async_remote_copy(
            src_ref=src, dst_ref=dst, send_sem=halo_send.at[i], recv_sem=halo_recv.at[i],
            device_id=at(lat_to, lon_to), device_id_type=MESH)

    beside = [
        halo(0, pack, right_m, lat, left),
        halo(1, pack, left_m, lat, right),
    ]
    to_up = [
        halo(2, spread.at[first, :], spread_b, above, lon),
        halo(3, temp.at[:, pl.ds(0, REACH), :], temp_b.at[:, pl.ds(0, REACH), :], above, lon),
        halo(4, pack.at[:, first, :], right_b, above, left),
        halo(5, pack.at[:, first, :], left_b, above, right),
    ]
    to_down = [
        halo(6, spread.at[last, :], spread_t, below, lon),
        halo(7, temp.at[:, pl.ds(rows - REACH, REACH), :],
             temp_t.at[:, pl.ds(PAD - REACH, REACH), :], below, lon),
        halo(8, pack.at[:, last, :], right_t, below, left),
        halo(9, pack.at[:, last, :], left_t, below, right),
    ]

    def clear(ref):
        ref[...] = jnp.zeros_like(ref)

    w0_p[feat:kp, :] = jnp.zeros((kp - feat, hid), jnp.float32)
    pad = own_x.shape[1] - feat
    for ref in (own_x, far_x):
        ref[:, feat:feat + pad, :] = jnp.zeros((half, pad, lanes), jnp.float32)

    @pl.when(jnp.logical_not(has_up))
    def _():
        for ref in (temp_t, spread_t, left_t, right_t):
            clear(ref)

    @pl.when(jnp.logical_not(has_down))
    def _():
        for ref in (temp_b, spread_b, left_b, right_b):
            clear(ref)

    for copy in small:
        copy.wait()

    def column(row):
        return jnp.broadcast_to(row, (lanes, row.shape[1])).T

    w0_p[0:feat, :] = w0t[...] * 0.5
    w0_c[...] = wide3(w0_p[...].T)
    b0_c[...] = column(b0[...] * 0.5)
    for k in range(depth):
        bm_c[k] = column(bm[k:k + 1, :] * 0.5)
    bf_c[...] = column(bf[...])
    large[0].wait()
    for k in range(depth):
        wm_c[k] = wide3(wm[k] * 0.5)
    large[1].wait()
    wf_c[...] = wide3(wf[...])

    large[2].wait()
    lane = lax.broadcasted_iota(jnp.int32, (rows, lanes), 1)
    for t in range(tiles):
        count = min(slots, levels - t * slots)
        acc = jnp.zeros((rows, lanes), jnp.float32)
        for m in range(count):
            moved = roll(temp_v[t * slots + m], EDGE * m + 2, 1)
            acc = jnp.where(lane // EDGE == m, moved, acc)
        pack[t] = acc
    acc = jnp.where(lane < EDGE, roll(spread_v[...], 2, 1), 0.0)
    step = EDGE
    while step < lanes:
        acc = acc + roll(acc, step, 1)
        step *= 2
    pack[tiles] = acc

    def wide(c):
        return jnp.concatenate([c] * GROUP, axis=1)

    def load(g):
        parts, suns = [], []
        for i in range(g * GROUP, (g + 1) * GROUP):
            on = lit[mine + i].astype(jnp.float32)
            x = own_x[i] * on + far_x[i] * (1.0 - on)
            parts.append(x)
            suns.append(x[2 * levels:2 * levels + 1, :])
        x = jnp.concatenate(parts, axis=1)
        tail = jnp.zeros((kp - x.shape[0], x.shape[1]), jnp.float32)
        return tall3(jnp.concatenate([x, tail], axis=0)), jnp.concatenate(suns, axis=1)

    def put(g, i):
        return pltpu.make_async_copy(
            res_own.at[i], heat.at[:, mine + i, :], put_sem.at[g])

    def send(g, i):
        return pltpu.make_async_remote_copy(
            src_ref=res_far.at[i], dst_ref=heat.at[:, mine + i, :],
            send_sem=out_send.at[g], recv_sem=out_recv.at[g],
            device_id=at(partner, lon), device_id_type=MESH)

    def finish(g, y, sun):
        y = (y + wide(bf_c[...])) * sun
        for j in range(GROUP):
            i = g * GROUP + j
            on = lit[mine + i].astype(jnp.float32)
            value = y[:, j * lanes:(j + 1) * lanes]
            res_far[i] = value * (1.0 - on)
            res_own[i] = value * on
            send(g, i).start()
            put(g, i).start()

    def activate(h, b):
        return tall3(gate(h + wide(b)))

    def pair(g, beside_it):
        a, sun_a = load(g)
        b, sun_b = load(g + 1)
        ya = dot(w0_c[...], a)
        yb = dot(w0_c[...], b)
        a = activate(ya, b0_c[...])
        beside_it(0)
        part = 1
        for k in range(depth):
            ya = dot(wm_c[k], a)
            b = activate(yb, b0_c[...] if k == 0 else bm_c[k - 1])
            beside_it(part)
            yb = dot(wm_c[k], b)
            a = activate(ya, bm_c[k])
            beside_it(part + 1)
            part += 2
        ya = dot(wf_c[...], a)
        b = activate(yb, bm_c[depth - 1])
        beside_it(part)
        finish(g, ya, sun_a)
        yb = dot(wf_c[...], b)
        finish(g + 1, yb, sun_b)

    def greet():
        @pl.when(leads)
        def _():
            pl.semaphore_wait(
                barrier, 2 + 3 * pair_up.astype(jnp.int32) + 3 * pair_down.astype(jnp.int32))
            pl.semaphore_signal(pair_sem, inc=1, device_id=at(partner, lon), device_id_type=MESH)

        @pl.when(jnp.logical_not(leads))
        def _():
            pl.semaphore_wait(pair_sem, 1)

        for copy in beside:
            copy.start()

        @pl.when(has_up)
        def _():
            for copy in to_up:
                copy.start()

        @pl.when(has_down)
        def _():
            for copy in to_down:
                copy.start()

    def early(part):
        if part == 2:
            greet()

    for g in range(2):
        own_wait(g)
        far_wait(g)
    pair(0, early)

    for copy in beside:
        copy.wait()

    @pl.when(has_up)
    def _():
        for copy in to_up:
            copy.wait_send()
        for copy in to_down:
            copy.wait_recv()

    @pl.when(has_down)
    def _():
        for copy in to_down:
            copy.wait_send()
        for copy in to_up:
            copy.wait_recv()

    tall = rows + 2 * PAD

    def stack(top, middle, bottom):
        return jnp.concatenate([top, middle, bottom], axis=0)

    def advance(x, f, west, east):
        around = roll(x, 1, 0) + roll(x, x.shape[0] - 1, 0) + west + east
        return x + f * (around - 4.0 * x)

    slot = lax.broadcasted_iota(jnp.int32, (tall, lanes), 1)
    where = lax.rem(slot, EDGE)
    zero8 = jnp.zeros((PAD, lanes), jnp.float32)

    def gather(t):
        lhs = stack(left_t[t], left_m[t], left_b[t])
        rhs = stack(right_t[t], right_m[t], right_b[t])
        here = stack(zero8, pack[t], zero8)
        return (jnp.where(where < 2, lhs, here), jnp.where(where < 2, here, rhs))

    f_west, f_east = gather(tiles)
    for t in range(tiles):
        west, east = gather(t)
        edge_0[t] = jnp.where(where == 1, roll(east, lanes - 1, 1), roll(west, 1, 1))
        west = advance(west, f_west, roll(west, 1, 1), roll(west, lanes - 1, 1))
        east = advance(east, f_east, roll(east, 1, 1), roll(east, lanes - 1, 1))
        edge_1[t] = jnp.where(where == 1, roll(east, lanes - 1, 1), roll(west, 1, 1))

    f_all[...] = stack(spread_t[...], spread_v[...], spread_b[...])

    def diffuse(k):
        t, m = k // slots, k % slots
        turn = lanes - 2 - EDGE * m
        x = stack(temp_t[k], temp_v[k], temp_b[k])
        rim = roll(edge_0[t], turn, 1)
        west = jnp.where(slot == 0, rim, roll(x, 1, 1))
        east = jnp.where(slot == lanes - 1, rim, roll(x, lanes - 1, 1))
        x = advance(x, f_all[...], west, east)
        core = x[PAD:PAD + rows]
        rim = roll(edge_1[t, PAD:PAD + rows], turn, 1)
        spot = slot[PAD:PAD + rows]
        west = jnp.where(spot == 0, rim, roll(core, 1, 1))
        east = jnp.where(spot == lanes - 1, rim, roll(core, lanes - 1, 1))
        north, south = roll(x, 1, 0)[PAD:PAD + rows], roll(x, tall - 1, 0)[PAD:PAD + rows]
        around = north + south + west + east
        nxt[k] = core + spread_v[...] * (around - 4.0 * core)

    def some(begin, end):
        for k in range(begin, end):
            diffuse(k)

    spread_over = 2 * depth + 2
    bulk = levels - min(TAIL, levels)

    def late(part):
        some(bulk * part // spread_over, bulk * (part + 1) // spread_over)

    for g in range(2, groups, 2):
        own_wait(g)
        own_wait(g + 1)
        far_wait(g)
        far_wait(g + 1)
        pair(g, late if g + 2 == groups else lambda part: None)
    some(bulk, levels)

    for g in range(groups):
        mine_g = res_far.at[pl.ds(g * GROUP, GROUP)]
        pltpu.make_async_remote_copy(
            src_ref=mine_g, dst_ref=mine_g, send_sem=out_send.at[g], recv_sem=out_recv.at[g],
            device_id=at(partner, lon), device_id_type=MESH).wait()
        pltpu.make_async_copy(mine_g, mine_g, put_sem.at[g]).wait()


PARTS = 3


def finish_kernel(heat, nxt, out_heat, out_temp, total, sem):
    levels = heat.shape[0]
    copies = []
    cuts = [levels * p // PARTS for p in range(PARTS + 1)]
    for p in range(PARTS):
        part = pl.ds(cuts[p], cuts[p + 1] - cuts[p])
        copies.append(pltpu.make_async_copy(heat.at[part], out_heat.at[part], sem.at[p]))
        copies[-1].start()
    for p in range(PARTS):
        part = pl.ds(cuts[p], cuts[p + 1] - cuts[p])
        total[part] = nxt[part] + heat[part]
        copies.append(pltpu.make_async_copy(total.at[part], out_temp.at[part], sem.at[PARTS + p]))
        copies[-1].start()
    for copy in copies:
        copy.wait()


def run(temp, moist, mu, lit, spread, w0, b0, wm, bm, wf, bf):
    levels, rows, lanes = temp.shape
    half = rows // 2
    hid = wm.shape[1]
    depth = wm.shape[0]
    feat = w0.shape[1]
    kp = up(feat, 256)
    tall = rows + 2 * PAD
    tiles = (levels * EDGE + lanes - 1) // lanes
    f32, bf16 = jnp.float32, jnp.bfloat16
    vmem = pl.BlockSpec(memory_space=pltpu.VMEM)
    hbm = pl.BlockSpec(memory_space=pltpu.HBM)
    groups = half // GROUP
    dma = pltpu.SemaphoreType.DMA

    def buf(*shape, dtype=f32):
        return pltpu.VMEM(shape, dtype)

    shape = jax.ShapeDtypeStruct(temp.shape, f32)
    heat, nxt = pl.pallas_call(
        kernel,
        out_shape=(shape, shape),
        in_specs=[hbm] * 11,
        out_specs=(vmem, vmem),
        scratch_shapes=[
            pltpu.SMEM((rows,), jnp.int32), buf(feat, hid), buf(1, hid), buf(*wm.shape),
            buf(*bm.shape), buf(*wf.shape), buf(1, levels),
            buf(levels, rows, lanes), buf(rows, lanes),
            buf(half, up(feat, 8), lanes), buf(half, up(feat, 8), lanes),
            buf(kp, hid), buf(hid, 3 * kp, dtype=bf16), buf(depth, hid, 3 * hid, dtype=bf16),
            buf(levels, 3 * hid, dtype=bf16),
            buf(hid, lanes), buf(depth, hid, lanes), buf(levels, lanes),
            buf(half, levels, lanes), buf(half, levels, lanes),
            buf(levels, PAD, lanes), buf(levels, PAD, lanes), buf(PAD, lanes), buf(PAD, lanes),
            buf(tiles + 1, rows, lanes),
            buf(tiles + 1, rows, lanes), buf(tiles + 1, PAD, lanes), buf(tiles + 1, PAD, lanes),
            buf(tiles + 1, rows, lanes), buf(tiles + 1, PAD, lanes), buf(tiles + 1, PAD, lanes),
            buf(tiles, tall, lanes), buf(tiles, tall, lanes), buf(tall, lanes),
            dma((9,)), dma((groups,)), dma((groups,)), dma((groups,)), dma((groups,)),
            dma((groups,)), dma((groups,)), dma((10,)), dma((10,)),
            pltpu.SemaphoreType.REGULAR,
        ],
        compiler_params=pltpu.CompilerParams(
            collective_id=0, has_side_effects=True, vmem_limit_bytes=48 << 20),
    )(*(
        pltpu.with_memory_space_constraint(x, pltpu.HBM)
        for x in (temp, moist, mu, lit, spread, w0.T, b0[None, :], wm, bm, wf, bf[None, :])
    ))
    return pl.pallas_call(
        finish_kernel,
        out_shape=(shape, shape),
        in_specs=[vmem, vmem],
        out_specs=(hbm, hbm),
        scratch_shapes=[buf(*temp.shape), dma((2 * PARTS,))],
        compiler_params=pltpu.CompilerParams(vmem_limit_bytes=8 << 20),
    )(heat, nxt)


def on_device(
    thermal_departure,
    moisture_profile,
    solar_elevation_factor,
    daylight_groups,
    spreading_factor,
    entry_layer_matrix,
    entry_layer_offset,
    inner_layer_matrices,
    inner_layer_offsets,
    final_layer_matrix,
    final_layer_offset,
):
    return run(
        thermal_departure,
        moisture_profile,
        solar_elevation_factor,
        daylight_groups[:, 0],
        spreading_factor,
        entry_layer_matrix,
        entry_layer_offset,
        inner_layer_matrices,
        inner_layer_offsets,
        final_layer_matrix,
        final_layer_offset,
    )


def solution(mesh):
    in_specs = (
        P(None, "lat", "lon"),
        P(None, "lat", "lon"),
        P("lat", "lon"),
        P("lat", "lon"),
        P("lat", "lon"),
        P(),
        P(),
        P(),
        P(),
        P(),
        P(),
    )
    out_specs = (P(None, "lat", "lon"), P(None, "lat", "lon"))
    return jax.shard_map(
        on_device, mesh=mesh, in_specs=in_specs, out_specs=out_specs, check_vma=False
    )
```

time: 29.3 us -> 27 us (0.922)
  other arithmetic: 1.43 us -> 0 us
  local copies, waits for them, and re-layouts: 1.11 us -> 0 us
    add x1 -> x0, other arithmetic: 1.43 us -> none  [on_device(): return (heating, state + heating)]
    unnamed x1 -> x0, local copies, waits for them, and re-layouts: 1.11 us -> none
    pallas_call x1 -> x2, Pallas kernels: 25.9 us -> 25.8 us  [the longest x1 24.2 us: run(): pl.pallas_call(kernel, out_shape=(shape, shape), in_specs=[hbm] * 11, out...]
where the time goes in v1:
time: 27 us; the launch traced here: 26.6 us
  Pallas kernels  25.8 us (96%)
  between operations  0.8 us (3%)
    pallas_call x1, Pallas kernels, run(): pl.pallas_call(kernel, out_shape=(shape, shape), in_specs=[hbm] * 11, out...  24.2 us
    pallas_call x1, Pallas kernels, run(): pl.pallas_call(finish_kernel, out_shape=(shape, shape), in_specs=[vmem, v...  1.64 us

profile of v1, /device:TPU:0, one launch (start us, length us, event | category | flops | bytes accessed | tf_op | source)
XLA Modules:
  0.0 26.6 jit_solution(14556704702739306134)
XLA Ops:
  0.6 24.2 %shard_map.122 = (f32[90,32,128]{2,1,0:T(8,128)S(1)}, f32[90,32,128]{2,1,0:T(8,128)S(1)}) custom-call(f32[90,32,128]{2,1,0:T(8,128)} %temp.1, f32[90,32,128]{2,1,0:T(8,128)} %moist.1, f32[32,128]{1,0:T(8,128)} %mu.1, s32[32]{0:T(128)} %bitcast.6, f32[32,128]{1,0:T(8,128)} %spread.1, f32[181,512]{1,0:T(8,128)} %bitcast.4, f32[1,512]{1,0:T(1,128)} %bitcast.5, ...), custom_call_target="tpu_custom_call" | custom-call | tf_op jit(solution)/shard_map/pallas_call | solution.py:477
  24.8 1.6 %shard_map.123 = (f32[90,32,128]{2,1,0:T(8,128)}, f32[90,32,128]{2,1,0:T(8,128)}) custom-call(f32[90,32,128]{2,1,0:T(8,128)S(1)} %get-tuple-element.4.heat, f32[90,32,128]{2,1,0:T(8,128)S(1)} %get-tuple-element.5.nxt), custom_call_target="tpu_custom_call" | custom-call | tf_op jit(solution)/shard_map/pallas_call | solution.py:506

commit v2 on v1

v2 whole, which is shorter than its diff:
```python
import jax
import jax.numpy as jnp
from jax import lax
from jax.experimental import pallas as pl
from jax.experimental.pallas import tpu as pltpu
from jax.sharding import PartitionSpec as P

MESH = pl.DeviceIdType.MESH
GROUP = 4
EDGE = 4
PAD = 8
REACH = 2
PREP_AT = 2
GREET_AT = 4
HALO_AT = 9
SPREAD = 5
TURNS = 8


def up(n, m):
    return (n + m - 1) // m * m


def split(x):
    hi = x.astype(jnp.bfloat16)
    lo = (x - hi.astype(jnp.float32)).astype(jnp.bfloat16)
    return hi, lo


def dot(a, b):
    return jnp.dot(a, b, preferred_element_type=jnp.float32)


def gate(h):
    return h + h * jnp.tanh(h)


def tall3(x):
    hi, lo = split(x)
    return jnp.concatenate([hi, lo, hi], axis=0)


def wide3(w):
    hi, lo = split(w)
    return jnp.concatenate([hi, hi, lo], axis=1)


def stacked(w):
    return jnp.concatenate(split(w), axis=0)


def dot3(w, x):
    hi, lo = split(x)
    n = w.shape[0] // 2
    both = dot(w, hi)
    return both[:n] + both[n:] + dot(w[:n], lo)


def roll(x, shift, axis):
    return pltpu.roll(x, shift % x.shape[axis], axis)


def kernel(
    temp, moist, mu, lit_h, spread, w0t_h, b0_h, wm_h, bm_h, wf_h, bf_h,
    heat, nxt,
    lit, w0t, b0, wm, bm, wf, bf,
    temp_v, spread_v, mu_v, mu_far, own_x, far_x,
    w0_p, w0_c, wm_c, wf_c, bm_c, bf_c,
    res_own, res_far,
    spread_t, spread_b,
    pack, left_m, left_t, left_b, right_m, right_t, right_b,
    rim, coef_0, coef_1, once,
    in_sem, own_sem, send_sem, recv_sem, put_sem, out_send, out_recv, halo_send, halo_recv,
    pair_sem,
):
    levels, rows, lanes = temp.shape
    half = rows // 2
    hid = wm_h.shape[1]
    depth = wm_h.shape[0]
    groups = half // GROUP
    feat = w0t_h.shape[0]
    kp = w0_c.shape[1]
    tiles = pack.shape[0] - 1
    slots = lanes // EDGE
    n_lat = lax.axis_size("lat")
    n_lon = lax.axis_size("lon")
    lat = lax.axis_index("lat")
    lon = lax.axis_index("lon")
    parity = lax.rem(lat, 2)
    partner = lat + 1 - 2 * parity
    mine = pl.multiple_of(parity * half, half)
    theirs = pl.multiple_of(half - parity * half, half)
    body = 2 * levels
    left = lax.rem(lon + n_lon - 1, n_lon)
    right = lax.rem(lon + 1, n_lon)
    has_up = lat > 0
    has_down = lat < n_lat - 1
    above = jnp.maximum(lat - 1, 0)
    below = jnp.minimum(lat + 1, n_lat - 1)
    leads = parity == 1
    pair_up = lat > 1
    pair_down = lat < n_lat - 2

    def at(lat_to, lon_to):
        return {"lat": lat_to, "lon": lon_to}

    def local(i, src, dst):
        return pltpu.make_async_copy(src, dst, in_sem.at[i])

    small = [
        local(0, w0t_h, w0t), local(1, lit_h, lit), local(2, b0_h, b0),
        local(3, bm_h, bm), local(4, bf_h, bf), local(5, spread, spread_v), local(6, mu, mu_v)]
    matrices = [local(7 + k, wm_h.at[k], wm.at[k]) for k in range(depth)]
    matrices.append(local(7 + depth, wf_h, wf))
    state = local(8 + depth, temp, temp_v.at[:, pl.ds(PAD, rows), :])

    def own_start(g):
        for i in range(g * GROUP, (g + 1) * GROUP):
            for src, begin in ((temp, 0), (moist, levels)):
                pltpu.make_async_copy(
                    src.at[:, mine + i, :], own_x.at[i, pl.ds(begin, levels), :],
                    own_sem.at[g]).start()

    def group_of(ref, g):
        return ref.at[pl.ds(g * GROUP, GROUP), pl.ds(0, body), :]

    def own_wait(g):
        block = group_of(own_x, g)
        pltpu.make_async_copy(block, block, own_sem.at[g]).wait()

    def swap(g, src, dst):
        return pltpu.make_async_remote_copy(
            src_ref=src, dst_ref=dst, send_sem=send_sem.at[g], recv_sem=recv_sem.at[g],
            device_id=at(partner, lon), device_id_type=MESH)

    sun_swap = swap(groups, mu.at[pl.ds(theirs, half), :], mu_far)

    def far_start(g):
        for i in range(g * GROUP, (g + 1) * GROUP):
            for src, begin in ((temp, 0), (moist, levels)):
                swap(g, src.at[:, theirs + i, :], far_x.at[i, pl.ds(begin, levels), :]).start()

    def far_wait(g):
        block = group_of(far_x, g)
        swap(g, block, block).wait()

    barrier = pltpu.get_barrier_semaphore()

    for copy in small:
        copy.start()

    @pl.when(leads)
    def _():
        pl.semaphore_signal(barrier, inc=1, device_id=at(partner, lon), device_id_type=MESH)

    own_start(0)
    own_start(1)

    @pl.when(jnp.logical_not(leads))
    def _():
        pl.semaphore_wait(barrier, 1)
        pl.semaphore_signal(pair_sem, inc=1, device_id=at(partner, lon), device_id_type=MESH)

    @pl.when(leads)
    def _():
        pl.semaphore_wait(pair_sem, 1)

        def hello(lat_to, lon_to):
            pl.semaphore_signal(
                barrier, inc=1, device_id=at(lat_to, lon_to), device_id_type=MESH)

        hello(lat, left)
        hello(lat, right)

        @pl.when(pair_up)
        def _():
            for to in (left, lon, right):
                hello(jnp.maximum(lat - 2, 0), to)

        @pl.when(pair_down)
        def _():
            for to in (left, lon, right):
                hello(jnp.minimum(lat + 2, n_lat - 1), to)

    far_start(0)
    sun_swap.start()
    far_start(1)
    for copy in matrices:
        copy.start()
    for g in range(2, groups):
        far_start(g)
        own_start(g)
    state.start()

    first, last = pl.ds(0, PAD), pl.ds(rows - PAD, PAD)

    def halo(i, src, dst, lat_to, lon_to):
        return pltpu.make_async_remote_copy(
            src_ref=src, dst_ref=dst, send_sem=halo_send.at[i], recv_sem=halo_recv.at[i],
            device_id=at(lat_to, lon_to), device_id_type=MESH)

    beside = [
        halo(0, pack, right_m, lat, left),
        halo(1, pack, left_m, lat, right),
    ]
    to_up = [
        halo(2, spread.at[first, :], spread_b, above, lon),
        halo(3, temp.at[:, pl.ds(0, REACH), :], temp_v.at[:, pl.ds(PAD + rows, REACH), :], above, lon),
        halo(4, pack.at[:, first, :], right_b, above, left),
        halo(5, pack.at[:, first, :], left_b, above, right),
    ]
    to_down = [
        halo(6, spread.at[last, :], spread_t, below, lon),
        halo(7, temp.at[:, pl.ds(rows - REACH, REACH), :],
             temp_v.at[:, pl.ds(PAD - REACH, REACH), :], below, lon),
        halo(8, pack.at[:, last, :], right_t, below, left),
        halo(9, pack.at[:, last, :], left_t, below, right),
    ]

    def clear(ref):
        ref[...] = jnp.zeros_like(ref)

    w0_p[feat:kp, :] = jnp.zeros((kp - feat, hid), jnp.float32)
    rest = own_x.shape[1] - feat
    for ref in (own_x, far_x):
        ref[:, feat:feat + rest, :] = jnp.where(
            lax.broadcasted_iota(jnp.int32, (half, rest, lanes), 1) == 0, 1.0, 0.0)

    @pl.when(jnp.logical_not(has_up))
    def _():
        temp_v[:, PAD - REACH:PAD, :] = jnp.zeros((levels, REACH, lanes), jnp.float32)
        for ref in (spread_t, left_t, right_t):
            clear(ref)

    @pl.when(jnp.logical_not(has_down))
    def _():
        temp_v[:, PAD + rows:PAD + rows + REACH, :] = jnp.zeros(
            (levels, REACH, lanes), jnp.float32)
        for ref in (spread_b, left_b, right_b):
            clear(ref)

    for copy in small:
        copy.wait()

    def column(row):
        return jnp.broadcast_to(row, (lanes, row.shape[1])).T

    w0_p[0:feat, :] = w0t[...] * 0.5
    w0_p[feat:feat + 1, :] = b0[...] * 0.5
    w0_c[...] = stacked(w0_p[...].T)
    for i in range(half):
        own_x[i, body:feat, :] = mu_v[pl.ds(mine + i, 1), :]

    def prepare(k):
        if k < depth:
            wm_c[k] = stacked(wm[k] * 0.5)
            bm_c[k] = column(bm[k:k + 1, :] * 0.5)
        else:
            wf_c[...] = wide3(wf[...])
            bf_c[...] = column(bf[...])

    def edges_of(x):
        at_lane = lax.broadcasted_iota(jnp.int32, x.shape, 1)
        acc = jnp.where(at_lane < EDGE, roll(x, 2, 1), 0.0)
        step = EDGE
        while step < lanes:
            acc = acc + roll(acc, step, 1)
            step *= 2
        return acc

    def pack_edges():
        lane = lax.broadcasted_iota(jnp.int32, (rows, lanes), 1)
        for t in range(tiles):
            count = min(slots, levels - t * slots)
            acc = jnp.zeros((rows, lanes), jnp.float32)
            for m in range(count):
                moved = roll(temp_v[t * slots + m, PAD:PAD + rows, :], EDGE * m + 2, 1)
                acc = jnp.where(lane // EDGE == m, moved, acc)
            pack[t] = acc
        pack[tiles] = edges_of(spread_v[...])

    def wide(c):
        return jnp.concatenate([c] * GROUP, axis=1)

    def load(g):
        parts, suns = [], []
        for i in range(g * GROUP, (g + 1) * GROUP):
            on = lit[mine + i].astype(jnp.float32)
            x = own_x[i] * on + far_x[i] * (1.0 - on)
            parts.append(x)
            suns.append(x[body:body + 1, :])
        x = jnp.concatenate(parts, axis=1)
        tail = jnp.zeros((kp - x.shape[0], x.shape[1]), jnp.float32)
        return jnp.concatenate([x, tail], axis=0), jnp.concatenate(suns, axis=1)

    def put(g, i):
        return pltpu.make_async_copy(
            res_own.at[i], heat.at[:, mine + i, :], put_sem.at[g])

    def send(g, i):
        return pltpu.make_async_remote_copy(
            src_ref=res_far.at[i], dst_ref=heat.at[:, mine + i, :],
            send_sem=out_send.at[g], recv_sem=out_recv.at[g],
            device_id=at(partner, lon), device_id_type=MESH)

    def finish(g, y, sun):
        y = (y + wide(bf_c[...])) * sun
        for j in range(GROUP):
            i = g * GROUP + j
            on = lit[mine + i].astype(jnp.float32)
            value = y[:, j * lanes:(j + 1) * lanes]
            res_far[i] = value * (1.0 - on)
            res_own[i] = value * on
            send(g, i).start()
            put(g, i).start()

    def greet():
        @pl.when(leads)
        def _():
            pl.semaphore_wait(
                barrier, 2 + 3 * pair_up.astype(jnp.int32) + 3 * pair_down.astype(jnp.int32))
            pl.semaphore_signal(pair_sem, inc=1, device_id=at(partner, lon), device_id_type=MESH)

        @pl.when(jnp.logical_not(leads))
        def _():
            pl.semaphore_wait(pair_sem, 1)

        for copy in beside:
            copy.start()

        @pl.when(has_up)
        def _():
            for copy in to_up:
                copy.start()

        @pl.when(has_down)
        def _():
            for copy in to_down:
                copy.start()

    tall = rows + 2 * PAD

    def stack(top, middle, bottom):
        return jnp.concatenate([top, middle, bottom], axis=0)

    def advance(x, f, west, east):
        around = roll(x, 1, 0) + roll(x, x.shape[0] - 1, 0) + west + east
        return x + f * (around - 4.0 * x)

    slot = lax.broadcasted_iota(jnp.int32, (tall, lanes), 1)
    where = lax.rem(slot, EDGE)
    zero8 = jnp.zeros((PAD, lanes), jnp.float32)

    def gather(t, here):
        lhs = stack(left_t[t], left_m[t], left_b[t])
        rhs = stack(right_t[t], right_m[t], right_b[t])
        return (jnp.where(where < 2, lhs, here), jnp.where(where < 2, here, rhs))

    def rows_ready():
        @pl.when(has_up)
        def _():
            for copy in to_down[:2]:
                copy.wait_recv()

        @pl.when(has_down)
        def _():
            for copy in to_up[:2]:
                copy.wait_recv()

        f = stack(spread_t[...], spread_v[...], spread_b[...])
        terms = (
            1.0 - 4.0 * f, f, jnp.where(slot == 0, 0.0, f), jnp.where(slot == lanes - 1, 0.0, f))
        span = coef_0.shape[1]
        for n, term in enumerate(terms):
            coef_0[n] = term[PAD - 1:PAD - 1 + span]
            coef_1[n] = term[PAD:PAD + rows]

    def sides_ready():
        for copy in beside:
            copy.wait_recv()

        @pl.when(has_up)
        def _():
            for copy in to_down[2:]:
                copy.wait_recv()

        @pl.when(has_down)
        def _():
            for copy in to_up[2:]:
                copy.wait_recv()

        f_west, f_east = gather(tiles, edges_of(stack(spread_t[...], spread_v[...], spread_b[...])))
        for t in range(tiles):
            west, east = gather(t, stack(zero8, pack[t], zero8))
            from_west, from_east = roll(west, 1, 1), roll(east, lanes - 1, 1)
            next_west = advance(west, f_west, from_west, roll(west, lanes - 1, 1))
            next_east = advance(east, f_east, roll(east, 1, 1), from_east)
            near_west = jnp.where(where == 2, f_west * from_west, 0.0)
            near_east = jnp.where(where == 1, f_east * from_east, 0.0)
            west = advance(near_west, f_west, roll(next_west, 1, 1), 0.0)
            east = advance(near_east, f_east, 0.0, roll(next_east, lanes - 1, 1))
            far_west = f_west * roll(near_west, 1, 1)
            far_east = f_east * roll(near_east, lanes - 1, 1)
            both = jnp.where(
                where < 2, jnp.where(where == 1, east, far_east),
                jnp.where(where == 2, west, far_west))
            rim[t] = both[PAD:PAD + rows]

    def spread_out(x, north, south, coef):
        return (
            x * coef[0] + (north + south) * coef[1]
            + roll(x, 1, 1) * coef[2] + roll(x, lanes - 1, 1) * coef[3])

    def diffuse(k):
        span = coef_0.shape[1]
        top = PAD - 1
        part = once.at[k % TURNS]
        part[0:span, :] = spread_out(
            temp_v[k, top:top + span, :], temp_v[k, top - 1:top - 1 + span, :],
            temp_v[k, top + 1:top + 1 + span, :], coef_0)
        nxt[k] = spread_out(
            part[1:1 + rows, :], part[0:rows, :], part[2:2 + rows, :], coef_1)

    outer = jnp.logical_or(slot[0:rows] < 2, slot[0:rows] >= lanes - 2)

    def correct(k):
        t, m = k // slots, k % slots
        turn = lanes - 2 - EDGE * m
        nxt[k] = nxt[k] + jnp.where(outer, roll(rim[t], turn, 1), 0.0)

    def some(begin, end):
        for k in range(begin, end):
            diffuse(k)

    order = [
        (g + s, layer) for g in range(0, groups, 2)
        for layer in range(depth + 2) for s in range(2)]

    def hook(event):
        if event < depth:
            prepare(event)
        if event == depth - 1:
            prepare(depth)
        if event == PREP_AT:
            state.wait()
            for g in range(2, groups):
                own_wait(g)
                far_wait(g)
            pack_edges()
        if event == GREET_AT:
            greet()
        if event == HALO_AT:
            rows_ready()
        part = event - HALO_AT
        if 0 <= part < SPREAD:
            some(levels * part // SPREAD, levels * (part + 1) // SPREAD)

    for g in range(2):
        own_wait(g)
        far_wait(g)
    sun_swap.wait()
    for copy in matrices:
        copy.wait()
    for i in range(half):
        far_x[i, body:feat, :] = mu_far[pl.ds(i, 1), :]

    suns, ready, pending = {}, {}, None

    def settle(g, layer, y):
        if layer <= depth:
            ready[g] = gate(y if layer == 0 else y + wide(bm_c[layer - 1]))
        else:
            finish(g, y, suns[g])

    for event, (g, layer) in enumerate(order):
        if layer == 0:
            ready[g], suns[g] = load(g)
        x = ready.pop(g)
        if layer == 0:
            y = dot3(w0_c[...], x)
        elif layer <= depth:
            y = dot3(wm_c[layer - 1], x)
        else:
            y = dot(wf_c[...], tall3(x))
        if pending is not None:
            settle(*pending)
        pending = (g, layer, y)
        hook(event)
    settle(*pending)
    sides_ready()
    for k in range(levels):
        correct(k)

    for copy in beside:
        copy.wait_send()

    @pl.when(has_up)
    def _():
        for copy in to_up:
            copy.wait_send()

    @pl.when(has_down)
    def _():
        for copy in to_down:
            copy.wait_send()

    for g in range(groups):
        mine_g = res_far.at[pl.ds(g * GROUP, GROUP)]
        pltpu.make_async_remote_copy(
            src_ref=mine_g, dst_ref=mine_g, send_sem=out_send.at[g], recv_sem=out_recv.at[g],
            device_id=at(partner, lon), device_id_type=MESH).wait()
        pltpu.make_async_copy(mine_g, mine_g, put_sem.at[g]).wait()


PARTS = 3


def finish_kernel(heat, nxt, out_heat, out_temp, total, sem):
    levels = heat.shape[0]
    copies = []
    cuts = [levels * p // PARTS for p in range(PARTS + 1)]
    for p in range(PARTS):
        part = pl.ds(cuts[p], cuts[p + 1] - cuts[p])
        copies.append(pltpu.make_async_copy(heat.at[part], out_heat.at[part], sem.at[p]))
        copies[-1].start()
    for p in range(PARTS):
        part = pl.ds(cuts[p], cuts[p + 1] - cuts[p])
        total[part] = nxt[part] + heat[part]
        copies.append(pltpu.make_async_copy(total.at[part], out_temp.at[part], sem.at[PARTS + p]))
        copies[-1].start()
    for copy in copies:
        copy.wait()


def run(temp, moist, mu, lit, spread, w0, b0, wm, bm, wf, bf):
    levels, rows, lanes = temp.shape
    half = rows // 2
    hid = wm.shape[1]
    depth = wm.shape[0]
    feat = w0.shape[1]
    kp = up(feat + 1, 256)
    tall = rows + 2 * PAD
    tiles = (levels * EDGE + lanes - 1) // lanes
    f32, bf16 = jnp.float32, jnp.bfloat16
    vmem = pl.BlockSpec(memory_space=pltpu.VMEM)
    hbm = pl.BlockSpec(memory_space=pltpu.HBM)
    groups = half // GROUP
    dma = pltpu.SemaphoreType.DMA

    def buf(*shape, dtype=f32):
        return pltpu.VMEM(shape, dtype)

    shape = jax.ShapeDtypeStruct(temp.shape, f32)
    heat, nxt = pl.pallas_call(
        kernel,
        out_shape=(shape, shape),
        in_specs=[hbm] * 11,
        out_specs=(vmem, vmem),
        scratch_shapes=[
            pltpu.SMEM((rows,), jnp.int32), buf(feat, hid), buf(1, hid), buf(*wm.shape),
            buf(*bm.shape), buf(*wf.shape), buf(1, levels),
            buf(levels, tall, lanes), buf(rows, lanes), buf(rows, lanes), buf(half, lanes),
            buf(half, up(feat + 1, 8), lanes), buf(half, up(feat + 1, 8), lanes),
            buf(kp, hid), buf(2 * hid, kp, dtype=bf16), buf(depth, 2 * hid, hid, dtype=bf16),
            buf(levels, 3 * hid, dtype=bf16),
            buf(depth, hid, lanes), buf(levels, lanes),
            buf(half, levels, lanes), buf(half, levels, lanes),
            buf(PAD, lanes), buf(PAD, lanes),
            buf(tiles + 1, rows, lanes),
            buf(tiles + 1, rows, lanes), buf(tiles + 1, PAD, lanes), buf(tiles + 1, PAD, lanes),
            buf(tiles + 1, rows, lanes), buf(tiles + 1, PAD, lanes), buf(tiles + 1, PAD, lanes),
            buf(tiles, rows, lanes), buf(4, rows + PAD, lanes), buf(4, rows, lanes),
            buf(TURNS, rows + PAD, lanes),
            dma((9 + depth,)), dma((groups,)), dma((groups + 1,)), dma((groups + 1,)), dma((groups,)),
            dma((groups,)), dma((groups,)), dma((10,)), dma((10,)),
            pltpu.SemaphoreType.REGULAR,
        ],
        compiler_params=pltpu.CompilerParams(
            collective_id=0, has_side_effects=True, vmem_limit_bytes=48 << 20),
    )(*(
        pltpu.with_memory_space_constraint(x, pltpu.HBM)
        for x in (temp, moist, mu, lit, spread, w0.T, b0[None, :], wm, bm, wf, bf[None, :])
    ))
    return pl.pallas_call(
        finish_kernel,
        out_shape=(shape, shape),
        in_specs=[vmem, vmem],
        out_specs=(hbm, hbm),
        scratch_shapes=[buf(*temp.shape), dma((2 * PARTS,))],
        compiler_params=pltpu.CompilerParams(vmem_limit_bytes=8 << 20),
    )(heat, nxt)


def on_device(
    thermal_departure,
    moisture_profile,
    solar_elevation_factor,
    daylight_groups,
    spreading_factor,
    entry_layer_matrix,
    entry_layer_offset,
    inner_layer_matrices,
    inner_layer_offsets,
    final_layer_matrix,
    final_layer_offset,
):
    return run(
        thermal_departure,
        moisture_profile,
        solar_elevation_factor,
        daylight_groups[:, 0],
        spreading_factor,
        entry_layer_matrix,
        entry_layer_offset,
        inner_layer_matrices,
        inner_layer_offsets,
        final_layer_matrix,
        final_layer_offset,
    )


def solution(mesh):
    in_specs = (
        P(None, "lat", "lon"),
        P(None, "lat", "lon"),
        P("lat", "lon"),
        P("lat", "lon"),
        P("lat", "lon"),
        P(),
        P(),
        P(),
        P(),
        P(),
        P(),
    )
    out_specs = (P(None, "lat", "lon"), P(None, "lat", "lon"))
    return jax.shard_map(
        on_device, mesh=mesh, in_specs=in_specs, out_specs=out_specs, check_vma=False
    )
```

time: 27 us -> 24.9 us (0.922)
  Pallas kernels: 25.8 us -> 23.9 us
    pallas_call x1, Pallas kernels: 24.2 us -> 22.3 us  [run(): pl.pallas_call(kernel, out_shape=(shape, shape), in_specs=[hbm] * 11, out...]
where the time goes in v2:
time: 24.9 us; the launch traced here: 24.7 us
  Pallas kernels  23.9 us (96%)
  between operations  0.8 us (3%)
    pallas_call x1, Pallas kernels, run(): pl.pallas_call(kernel, out_shape=(shape, shape), in_specs=[hbm] * 11, out...  22.3 us
    pallas_call x1, Pallas kernels, run(): pl.pallas_call(finish_kernel, out_shape=(shape, shape), in_specs=[vmem, v...  1.64 us

profile of v2, /device:TPU:0, one launch (start us, length us, event | category | flops | bytes accessed | tf_op | source)
XLA Modules:
  0.0 24.7 jit_solution(17496364147073608637)
XLA Ops:
  0.6 22.3 %shard_map.122 = (f32[90,32,128]{2,1,0:T(8,128)S(1)}, f32[90,32,128]{2,1,0:T(8,128)S(1)}) custom-call(f32[90,32,128]{2,1,0:T(8,128)} %temp.1, f32[90,32,128]{2,1,0:T(8,128)} %moist.1, f32[32,128]{1,0:T(8,128)} %mu.1, s32[32]{0:T(128)} %bitcast.6, f32[32,128]{1,0:T(8,128)} %spread.1, f32[181,512]{1,0:T(8,128)} %bitcast.4, f32[1,512]{1,0:T(1,128)} %bitcast.5, ...), custom_call_target="tpu_custom_call" | custom-call | tf_op jit(solution)/shard_map/pallas_call | solution.py:554
  22.9 1.6 %shard_map.123 = (f32[90,32,128]{2,1,0:T(8,128)}, f32[90,32,128]{2,1,0:T(8,128)}) custom-call(f32[90,32,128]{2,1,0:T(8,128)S(1)} %get-tuple-element.4.heat, f32[90,32,128]{2,1,0:T(8,128)S(1)} %get-tuple-element.5.nxt), custom_call_target="tpu_custom_call" | custom-call | tf_op jit(solution)/shard_map/pallas_call | solution.py:584

commit v3 on v2

--- a/solution.py
+++ b/solution.py
@@ -10,10 +10,10 @@
 EDGE = 4
 PAD = 8
 REACH = 2
-PREP_AT = 2
-GREET_AT = 4
-HALO_AT = 9
-SPREAD = 5
+PREP_AT = 0
+GREET_AT = 1
+HALO_AT = 6
+SPREAD = 8
 TURNS = 8
 
 
@@ -69,7 +69,7 @@
     res_own, res_far,
     spread_t, spread_b,
     pack, left_m, left_t, left_b, right_m, right_t, right_b,
-    rim, coef_0, coef_1, once,
+    rim, coef_0, coef_1, once, spread_e,
     in_sem, own_sem, send_sem, recv_sem, put_sem, out_send, out_recv, halo_send, halo_recv,
     pair_sem,
 ):
@@ -370,6 +370,7 @@
         f = stack(spread_t[...], spread_v[...], spread_b[...])
         terms = (
             1.0 - 4.0 * f, f, jnp.where(slot == 0, 0.0, f), jnp.where(slot == lanes - 1, 0.0, f))
+        spread_e[...] = edges_of(f)
         span = coef_0.shape[1]
         for n, term in enumerate(terms):
             coef_0[n] = term[PAD - 1:PAD - 1 + span]
@@ -389,7 +390,7 @@
             for copy in to_up[2:]:
                 copy.wait_recv()
 
-        f_west, f_east = gather(tiles, edges_of(stack(spread_t[...], spread_v[...], spread_b[...])))
+        f_west, f_east = gather(tiles, spread_e[...])
         for t in range(tiles):
             west, east = gather(t, stack(zero8, pack[t], zero8))
             from_west, from_east = roll(west, 1, 1), roll(east, lanes - 1, 1)
@@ -570,7 +571,7 @@
             buf(tiles + 1, rows, lanes), buf(tiles + 1, PAD, lanes), buf(tiles + 1, PAD, lanes),
             buf(tiles + 1, rows, lanes), buf(tiles + 1, PAD, lanes), buf(tiles + 1, PAD, lanes),
             buf(tiles, rows, lanes), buf(4, rows + PAD, lanes), buf(4, rows, lanes),
-            buf(TURNS, rows + PAD, lanes),
+            buf(TURNS, rows + PAD, lanes), buf(tall, lanes),
             dma((9 + depth,)), dma((groups,)), dma((groups + 1,)), dma((groups + 1,)), dma((groups,)),
             dma((groups,)), dma((groups,)), dma((10,)), dma((10,)),
             pltpu.SemaphoreType.REGULAR,

time: 24.9 us -> 23.5 us (0.944)
  Pallas kernels: 23.9 us -> 22.5 us
    pallas_call x1, Pallas kernels: 22.3 us -> 20.9 us  [run(): pl.pallas_call(kernel, out_shape=(shape, shape), in_specs=[hbm] * 11, out...]
where the time goes in v3:
time: 23.5 us; the launch traced here: 23.3 us
  Pallas kernels  22.5 us (96%)
  between operations  0.8 us (3%)
    pallas_call x1, Pallas kernels, run(): pl.pallas_call(kernel, out_shape=(shape, shape), in_specs=[hbm] * 11, out...  20.9 us
    pallas_call x1, Pallas kernels, run(): pl.pallas_call(finish_kernel, out_shape=(shape, shape), in_specs=[vmem, v...  1.64 us

profile of v3, /device:TPU:0, one launch (start us, length us, event | category | flops | bytes accessed | tf_op | source)
XLA Modules:
  0.0 23.3 jit_solution(11948250750247066562)
XLA Ops:
  0.6 20.9 %shard_map.122 = (f32[90,32,128]{2,1,0:T(8,128)S(1)}, f32[90,32,128]{2,1,0:T(8,128)S(1)}) custom-call(f32[90,32,128]{2,1,0:T(8,128)} %temp.1, f32[90,32,128]{2,1,0:T(8,128)} %moist.1, f32[32,128]{1,0:T(8,128)} %mu.1, s32[32]{0:T(128)} %bitcast.6, f32[32,128]{1,0:T(8,128)} %spread.1, f32[181,512]{1,0:T(8,128)} %bitcast.4, f32[1,512]{1,0:T(1,128)} %bitcast.5, ...), custom_call_target="tpu_custom_call" | custom-call | tf_op jit(solution)/shard_map/pallas_call | solution.py:555
  21.5 1.6 %shard_map.123 = (f32[90,32,128]{2,1,0:T(8,128)}, f32[90,32,128]{2,1,0:T(8,128)}) custom-call(f32[90,32,128]{2,1,0:T(8,128)S(1)} %get-tuple-element.4.heat, f32[90,32,128]{2,1,0:T(8,128)S(1)} %get-tuple-element.5.nxt), custom_call_target="tpu_custom_call" | custom-call | tf_op jit(solution)/shard_map/pallas_call | solution.py:585

commit v4 on v3

--- a/solution.py
+++ b/solution.py
@@ -187,10 +187,10 @@
     far_start(1)
     for copy in matrices:
         copy.start()
+    state.start()
     for g in range(2, groups):
         far_start(g)
         own_start(g)
-    state.start()
 
     first, last = pl.ds(0, PAD), pl.ds(rows - PAD, PAD)
 
@@ -444,10 +444,11 @@
             prepare(depth)
         if event == PREP_AT:
             state.wait()
+            pack_edges()
+        if event == HALO_AT:
             for g in range(2, groups):
                 own_wait(g)
                 far_wait(g)
-            pack_edges()
         if event == GREET_AT:
             greet()
         if event == HALO_AT:

time: 23.5 us -> 23.4 us (level)
  no operation moved by 1% of the time
where the time goes in v4:
time: 23.4 us; the launch traced here: 23.3 us
  Pallas kernels  22.4 us (96%)
  between operations  0.8 us (3%)
    pallas_call x1, Pallas kernels, run(): pl.pallas_call(kernel, out_shape=(shape, shape), in_specs=[hbm] * 11, out...  20.8 us
    pallas_call x1, Pallas kernels, run(): pl.pallas_call(finish_kernel, out_shape=(shape, shape), in_specs=[vmem, v...  1.64 us

profile of v4, /device:TPU:0, one launch (start us, length us, event | category | flops | bytes accessed | tf_op | source)
XLA Modules:
  0.0 23.3 jit_solution(17805420077236432707)
XLA Ops:
  0.6 20.8 %shard_map.122 = (f32[90,32,128]{2,1,0:T(8,128)S(1)}, f32[90,32,128]{2,1,0:T(8,128)S(1)}) custom-call(f32[90,32,128]{2,1,0:T(8,128)} %temp.1, f32[90,32,128]{2,1,0:T(8,128)} %moist.1, f32[32,128]{1,0:T(8,128)} %mu.1, s32[32]{0:T(128)} %bitcast.6, f32[32,128]{1,0:T(8,128)} %spread.1, f32[181,512]{1,0:T(8,128)} %bitcast.4, f32[1,512]{1,0:T(1,128)} %bitcast.5, ...), custom_call_target="tpu_custom_call" | custom-call | tf_op jit(solution)/shard_map/pallas_call | solution.py:556
  21.4 1.6 %shard_map.123 = (f32[90,32,128]{2,1,0:T(8,128)}, f32[90,32,128]{2,1,0:T(8,128)}) custom-call(f32[90,32,128]{2,1,0:T(8,128)S(1)} %get-tuple-element.4.heat, f32[90,32,128]{2,1,0:T(8,128)S(1)} %get-tuple-element.5.nxt), custom_call_target="tpu_custom_call" | custom-call | tf_op jit(solution)/shard_map/pallas_call | solution.py:586
